TPU v7x, 32 devices: a whole 2x2x4 slice. The times are simulated.
32 devices in a mesh: dp: 2 (over x), ctx: 16 (over z, y, core).
Axes of the slice: x: 2, y: 2, z: 4, core: 2. Of those that a mesh axis runs over, the one named last changes fastest.
Arguments:
- token_ids: int32 [2, 2048], P('dp', 'ctx'), may hold values from 0 to 7
- queries: bfloat16 [2, 2048, 4096], P('dp', 'ctx'), may hold values from -6 to 6
- gated_values: bfloat16 [2, 2048, 4096], P('dp', 'ctx'), may hold values from -6 to 6
- out_grad: bfloat16 [2, 2048, 4096], P('dp', 'ctx'), may hold values from -6 to 6
- filters: bfloat16 [4096, 128], P('ctx'), may hold values from -0.5 to 0.5
Outputs:
- value_grad: bfloat16 [2, 2048, 4096], P('dp', 'ctx')
- filter_grad: float32 [4096, 128], P('ctx')
Inputs may be any that keep to these rules, and one draw needn't show every extreme that they name: `token_ids`: ids 0 to 3 are upper-case bases, 4 to 7 lower-case bases.
All inputs are finite; a program needn't handle non-finite values.
Results may differ from a plain program's by a relative error of at most 0.0049.
Values may be sent and summed in bfloat16 or wider, within the bound.
No kernel may reach another device: no remote copies, remote signals or barrier semaphores. Data moves between devices by JAX's collectives and lax.ppermute only.
A program may use at most 64 MiB of HBM per device.

v0:
```python
import jax
import jax.numpy as jnp
from jax import lax
from jax.sharding import PartitionSpec as P


def shifted(x, axis, by):
    length = lax.axis_size(axis)
    pairs = [(i, i + by) for i in range(length) if 0 <= i + by < length]
    return lax.ppermute(x, axis, pairs)


def correlate(signal, kernel):
    channels = signal.shape[2]
    return lax.conv_general_dilated(
        signal,
        kernel[:, None, :],
        (1,),
        "VALID",
        dimension_numbers=("NWC", "WIO", "NWC"),
        feature_group_count=channels,
        preferred_element_type=jnp.float32,
    )


def body(token_ids, queries, gated_values, out_grad, filters):
    weight = jnp.where(token_ids < 4, 1.0, 0.1).astype(jnp.float32)
    cotangent = (
        weight[:, :, None] * out_grad.astype(jnp.float32) * queries.astype(jnp.float32)
    ).astype(jnp.bfloat16)
    tap_count = filters.shape[1]
    token_total = lax.axis_size("dp") * lax.axis_size("ctx") * queries.shape[1]
    factor_tok = float(token_total) ** (-0.5)
    next_part = shifted(cotangent[:, : tap_count - 1], "ctx", -1)
    signal = jnp.concatenate([cotangent, next_part], axis=1)
    all_filters = lax.all_gather(filters, "ctx", axis=0, tiled=True)
    value_grad = correlate(signal, all_filters.T).astype(jnp.bfloat16)
    values_wide = gated_values[0]
    local_taps = lax.psum_scatter(
        correlate(signal, values_wide)[0].T * factor_tok, "ctx", scatter_dimension=0, tiled=True
    )
    filter_grad = lax.psum(local_taps, "dp")
    return (value_grad, filter_grad)


def solution(mesh):
    return jax.shard_map(
        body,
        mesh=mesh,
        in_specs=(
            P("dp", "ctx"),
            P("dp", "ctx", None),
            P("dp", "ctx", None),
            P("dp", "ctx", None),
            P("ctx", None),
        ),
        out_specs=(P("dp", "ctx", None), P("ctx", None)),
        check_vma=False,
    )
```

profile of v0, /device:TPU:0, one launch (start us, length us, event | category | flops | bytes accessed | tf_op | source)
XLA Modules:
  0.0 201.7 jit_solution(6966847847205426817)
XLA Ops:
  7.2 0.0 copy-start
  7.2 0.0 reduce-scatter.2.cloned.1.call-start
  7.2 0.7 fusion.4
  8.0 2.0 multiply_convert_fusion
  10.0 1.3 collective-permute-start
  11.3 3.3 %collective-permute-done = bf16[1,127,4096]{2,1,0:T(8,128)(2,1)S(1)} collective-permute-done((bf16[1,127,4096]{2,1,0:T(8,128)(2,1)S(1)}, bf16[1,127,4096]{2,1,0:T(8,128)(2,1)S(1)}, u32[]{:S(2)}, u32[]{:S(2)}) %collective-permute-start) | collective-permute-done | bytes 1040416 | tf_op jit(solution)/shard_map/ppermute | solution.py:10
  14.5 0.2 pad_maximum_fusion
  14.7 0.0 copy-done
  14.7 30.5 %convolution_multiply_fusion = f32[1,128,4096]{2,0,1:T(1,128)S(1)} fusion(bf16[1,255,4096]{2,1,0:T(8,128)(2,1)S(1)} %pad_maximum_fusion, bf16[128,1,4096]{2,0,1:T(8,128)(2,1)S(1)} %bitcast.12), kind=kOutput, calls=%fused_computation.1 | convolution fusion | flops 134742016 | bytes 5234688 | tf_op jit(solution)/shard_map/conv_general_dilated | solution.py:15
  45.3 3.0 %copy.46 = f32[1,128,4096]{2,1,0:T(8,128)} copy(f32[1,128,4096]{2,0,1:T(1,128)S(1)} %convolution_multiply_fusion) | data formatting | bytes 4194304
  48.3 0.0 copy-start.1
  48.3 0.0 reduce-scatter.2.cloned.1.call-update
  48.3 0.0 all-gather.2.cloned.1.call-start
  48.4 0.8 copy-done.1
  49.1 0.7 copy.29
  49.9 0.0 all-gather.2.cloned.1.call-update
  49.9 0.0 all-reduce.2.cloned.1.call-start
  49.9 74.0 %reduce-scatter.2.cloned.1.call-done = f32[256,128]{0,1:T(8,128)} async-done(((f32[4096,128]{0,1:T(8,128)}), f32[256,128]{0,1:T(8,128)}) %reduce-scatter.2.cloned.1.call-update) | async-done | bytes 131088 | tf_op jit(solution)/shard_map/reduce_scatter | solution.py:39
  124.0 0.0 all-reduce.2.cloned.1.call-update
  124.0 38.3 %all-gather.2.cloned.1.call-done = bf16[4096,128]{0,1:T(8,128)(2,1)} async-done(((bf16[256,128]{0,1:T(8,128)(2,1)}), bf16[4096,128]{0,1:T(8,128)(2,1)}) %all-gather.2.cloned.1.call-update) | async-done | bytes 1048592 | tf_op jit(solution)/shard_map/all_gather | solution.py:36
  162.3 29.1 %convolution_convert_fusion = bf16[1,128,4096]{2,0,1:T(2,128)(2,1)S(1)} fusion(bf16[1,255,4096]{2,1,0:T(8,128)(2,1)S(1)} %pad_maximum_fusion, bf16[128,1,4096]{2,0,1:T(8,128)(2,1)} %bitcast.15), kind=kOutput, calls=%fused_computation | convolution fusion | flops 134742016 | bytes 4186112 | tf_op jit(solution)/shard_map/conv_general_dilated | solution.py:15
  191.4 2.1 %copy.34 = bf16[1,128,4096]{2,1,0:T(8,128)(2,1)} copy(bf16[1,128,4096]{2,0,1:T(2,128)(2,1)S(1)} %convolution_convert_fusion) | data formatting | bytes 2097152
  193.5 0.0 all-reduce.2.cloned.1.call-done
  193.5 1.7 copy.35
Async XLA Ops:
  7.2 7.6 %copy-start = (bf16[1,128,4096]{2,1,0:T(8,128)(2,1)S(1)}, bf16[1,128,4096]{2,1,0:T(8,128)(2,1)}, u32[]{:S(2)}) copy-start(bf16[1,128,4096]{2,1,0:T(8,128)(2,1)} %param.7) | copy-start | bytes 3145732
  7.2 116.8 %reduce-scatter.2.cloned.1.call-start = ((), (), s32[]{:S(2)}) async-start(), calls=%async_computation.2 | async-start | bytes 2228224 | tf_op jit(solution)/shard_map/reduce_scatter | solution.py:39
  10.0 4.6 %collective-permute-start = (bf16[1,127,4096]{2,1,0:T(8,128)(2,1)S(1)}, bf16[1,127,4096]{2,1,0:T(8,128)(2,1)S(1)}, u32[]{:S(2)}, u32[]{:S(2)}) collective-permute-start(bf16[1,127,4096]{2,1,0:T(8,128)(2,1)S(1)} %bitcast.14), channel_id=1, source_target_pairs={{1,0},{2,1},{3,2},{4,3},{5,4},{6,5},{7,6},{8,7},{9,8},{10,9},{11,1... | collective-permute-start | bytes 3121160 | tf_op jit(solution)/shard_map/ppermute | solution.py:10
  48.3 0.8 copy-start.1
  48.3 114.0 %all-gather.2.cloned.1.call-start = ((), (), s32[]{:S(2)}) async-start(), calls=%async_computation.1 | async-start | bytes 1114112 | tf_op jit(solution)/shard_map/all_gather | solution.py:36
  49.9 143.6 %all-reduce.2.cloned.1.call-start = ((), (), s32[]{:S(2)}) async-start(), calls=%async_computation.3 | async-start | bytes 262144 | tf_op jit(solution)/shard_map/psum | solution.py:42
Sparse Core Ops, SparseCore 0:
  48.4 75.4 reduce-scatter.1
  126.7 35.5 all-gather.1
  164.6 21.1 all-reduce.1
where the time goes:
time: 202 us
  waiting for transfers between devices  116 us (57%)
  matrix products  59.6 us (30%)
  between operations  13.8 us (7%)
  local copies, waits for them, and re-layouts  8.28 us (4%)
  other arithmetic  2.94 us (1%)
    reduce_scatter x1, waiting for transfers between devices, body(): lax.psum_scatter(correlate(signal, values_wide)[0].T * factor_tok, 'ctx',...  74 us
    conv_general_dilated x2, matrix products, correlate(): lax.conv_general_dilated(signal, kernel[:, None, :], (1,), 'VALID', dimen...  59.6 us
    all_gather x1, waiting for transfers between devices, body(): all_filters = lax.all_gather(filters, 'ctx', axis=0, tiled=True)  38.3 us
    unnamed x8, local copies, waits for them, and re-layouts  8.28 us
  transfers between devices with their start and end apart: 4, of which 3 were waited for; matrix products, arithmetic and copies ran while one was open for 16% of the time, Pallas kernels for 0%

commit v1 on v0

--- a/solution.py
+++ b/solution.py
@@ -33,7 +33,17 @@
     factor_tok = float(token_total) ** (-0.5)
     next_part = shifted(cotangent[:, : tap_count - 1], "ctx", -1)
     signal = jnp.concatenate([cotangent, next_part], axis=1)
-    all_filters = lax.all_gather(filters, "ctx", axis=0, tiled=True)
+    size, position, extent = (lax.axis_size("ctx"), lax.axis_index("ctx"), filters.shape[0])
+    upward = [(i_2, (i_2 + 1) % size) for i_2 in range(size)]
+    all_filters = jnp.zeros(
+        (*filters.shape[:0], size * extent, *filters.shape[0 + 1 :]), filters.dtype
+    )
+    held = filters
+    for step in range(size):
+        source = (position - step) % size
+        all_filters = lax.dynamic_update_slice_in_dim(all_filters, held, source * extent, axis=0)
+        if step < size - 1:
+            held = lax.ppermute(held, "ctx", upward)
     value_grad = correlate(signal, all_filters.T).astype(jnp.bfloat16)
     values_wide = gated_values[0]
     local_taps = lax.psum_scatter(

time: 202 us -> 198 us (0.980)
  waiting for transfers between devices: 116 us -> 87.4 us
  starting transfers between devices: 1.41 us -> 14.8 us
  local copies, waits for them, and re-layouts: 8.28 us -> 18.8 us
    ppermute x0 -> x15, waiting for transfers between devices: none -> 84.1 us  [body(): held = lax.ppermute(held, 'ctx', upward)]
    reduce_scatter x1, waiting for transfers between devices: 74 us -> 0.01 us  [body(): lax.psum_scatter(correlate(signal, values_wide)[0].T * factor_tok, 'ctx',...]
    all_gather x1 -> x0, waiting for transfers between devices: 38.3 us -> none  [body(): all_filters = lax.all_gather(filters, 'ctx', axis=0, tiled=True)]
    ppermute x0 -> x15, starting transfers between devices: none -> 13.4 us  [body(): held = lax.ppermute(held, 'ctx', upward)]
    dynamic_update_slice x0 -> x16, local copies, waits for them, and re-layouts: none -> 10.1 us  [body(): lax.dynamic_update_slice_in_dim(all_filters, held, source * extent, axis=0)]
  transfers between devices with their start and end apart: 4 -> 18, of which waited for: 3 -> 15; matrix products, arithmetic and copies ran while one was open for 16% -> 22% of each run, Pallas kernels for 0% -> 0%
where the time goes in v1:
time: 198 us
  waiting for transfers between devices  87.4 us (44%)
  matrix products  59.6 us (30%)
  local copies, waits for them, and re-layouts  18.8 us (9%)
  starting transfers between devices  14.8 us (7%)
  between operations  14.1 us (7%)
  other arithmetic  2.94 us (1%)
    ppermute x15, waiting for transfers between devices, body(): held = lax.ppermute(held, 'ctx', upward)  84.1 us
    conv_general_dilated x2, matrix products, correlate(): lax.conv_general_dilated(signal, kernel[:, None, :], (1,), 'VALID', dimen...  59.6 us
    ppermute x15, starting transfers between devices, body(): held = lax.ppermute(held, 'ctx', upward)  13.4 us
    dynamic_update_slice x16, local copies, waits for them, and re-layouts, body(): lax.dynamic_update_slice_in_dim(all_filters, held, source * extent, axis=0)  10.1 us
    unnamed x8, local copies, waits for them, and re-layouts  7.63 us
  transfers between devices with their start and end apart: 18, of which 15 were waited for; matrix products, arithmetic and copies ran while one was open for 22% of the time, Pallas kernels for 0%

profile of v1, /device:TPU:0, one launch (start us, length us, event | category | flops | bytes accessed | tf_op | source)
XLA Modules:
  0.0 197.7 jit_solution(5517771045459071581)
XLA Ops:
  7.2 0.7 fusion.4
  8.0 2.0 %multiply_convert_fusion = bf16[1,128,4096]{2,1,0:T(8,128)(2,1)S(1)} fusion(bf16[1,128,4096]{2,1,0:T(8,128)(2,1)} %param.6, bf16[1,128,4096]{2,1,0:T(8,128)(2,1)} %param.8, f32[128]{0:T(128)S(1)} %fusion.4), kind=kLoop, calls=%fused_computation.8 | loop fusion | flops 2621440 | bytes 3146240 | tf_op jit(solution)/shard_map/convert_element_type | solution.py:30
  10.0 1.3 collective-permute-start
  11.3 3.3 %collective-permute-done = bf16[1,127,4096]{2,1,0:T(8,128)(2,1)S(1)} collective-permute-done((bf16[1,127,4096]{2,1,0:T(8,128)(2,1)S(1)}, bf16[1,127,4096]{2,1,0:T(8,128)(2,1)S(1)}, u32[]{:S(2)}, u32[]{:S(2)}) %collective-permute-start) | collective-permute-done | bytes 1040416 | tf_op jit(solution)/shard_map/ppermute | solution.py:10
  14.7 30.5 %convolution_multiply_fusion = f32[1,128,4096]{2,0,1:T(1,128)S(1)} fusion(bf16[1,255,4096]{2,1,0:T(8,128)(2,1)S(1)} %pad_maximum_fusion, bf16[128,1,4096]{2,0,1:T(8,128)(2,1)S(1)} %bitcast.12), kind=kOutput, calls=%fused_computation.1 | convolution fusion | flops 134742016 | bytes 5234688 | tf_op jit(solution)/shard_map/conv_general_dilated | solution.py:15
  45.3 3.0 %copy.64 = f32[1,128,4096]{2,1,0:T(8,128)} copy(f32[1,128,4096]{2,0,1:T(1,128)S(1)} %convolution_multiply_fusion) | data formatting | bytes 4194304
  48.3 0.8 copy-done.1
  49.2 13.0 %collective-permute-start.1 = (bf16[256,128]{0,1:T(8,128)(2,1)S(1)}, bf16[256,128]{0,1:T(8,128)(2,1)S(1)}, u32[]{:S(2)}, u32[]{:S(2)}) collective-permute-start(bf16[256,128]{0,1:T(8,128)(2,1)S(1)} %copy.46), channel_id=1, source_target_pairs={{0,1},{1,2},{2,3},{3,4},{4,5},{5,6},{6,7},{7,8},{8,9},{9,10},{10,1... | collective-permute-start | bytes 196616 | tf_op jit(solution)/shard_map/ppermute | solution.py:46
  62.2 1.1 broadcast_in_dim.17
  64.9 5.4 %collective-permute-done.2 = bf16[256,128]{0,1:T(8,128)(2,1)S(1)} collective-permute-done((bf16[256,128]{0,1:T(8,128)(2,1)S(1)}, bf16[256,128]{0,1:T(8,128)(2,1)S(1)}, u32[]{:S(2)}, u32[]{:S(2)}) %collective-permute-start.2) | collective-permute-done | bytes 65568 | tf_op jit(solution)/shard_map/ppermute | solution.py:46
  70.3 0.6 constant_dynamic-update-slice_fusion.13
  71.0 5.8 %collective-permute-done.3 = bf16[256,128]{0,1:T(8,128)(2,1)S(1)} collective-permute-done((bf16[256,128]{0,1:T(8,128)(2,1)S(1)}, bf16[256,128]{0,1:T(8,128)(2,1)S(1)}, u32[]{:S(2)}, u32[]{:S(2)}) %collective-permute-start.3) | collective-permute-done | bytes 65568 | tf_op jit(solution)/shard_map/ppermute | solution.py:46
  76.7 0.6 constant_dynamic-update-slice_fusion.12
  77.3 5.8 %collective-permute-done.4 = bf16[256,128]{0,1:T(8,128)(2,1)S(1)} collective-permute-done((bf16[256,128]{0,1:T(8,128)(2,1)S(1)}, bf16[256,128]{0,1:T(8,128)(2,1)S(1)}, u32[]{:S(2)}, u32[]{:S(2)}) %collective-permute-start.4) | collective-permute-done | bytes 65568 | tf_op jit(solution)/shard_map/ppermute | solution.py:46
  83.1 0.6 constant_dynamic-update-slice_fusion.11
  83.7 5.8 %collective-permute-done.5 = bf16[256,128]{0,1:T(8,128)(2,1)S(1)} collective-permute-done((bf16[256,128]{0,1:T(8,128)(2,1)S(1)}, bf16[256,128]{0,1:T(8,128)(2,1)S(1)}, u32[]{:S(2)}, u32[]{:S(2)}) %collective-permute-start.5) | collective-permute-done | bytes 65568 | tf_op jit(solution)/shard_map/ppermute | solution.py:46
  89.5 0.6 constant_dynamic-update-slice_fusion.10
  90.1 7.0 %collective-permute-done.6 = bf16[256,128]{0,1:T(8,128)(2,1)S(1)} collective-permute-done((bf16[256,128]{0,1:T(8,128)(2,1)S(1)}, bf16[256,128]{0,1:T(8,128)(2,1)S(1)}, u32[]{:S(2)}, u32[]{:S(2)}) %collective-permute-start.6) | collective-permute-done | bytes 65568 | tf_op jit(solution)/shard_map/ppermute | solution.py:46
  97.1 0.6 constant_dynamic-update-slice_fusion.9
  97.7 7.0 %collective-permute-done.7 = bf16[256,128]{0,1:T(8,128)(2,1)S(1)} collective-permute-done((bf16[256,128]{0,1:T(8,128)(2,1)S(1)}, bf16[256,128]{0,1:T(8,128)(2,1)S(1)}, u32[]{:S(2)}, u32[]{:S(2)}) %collective-permute-start.7) | collective-permute-done | bytes 65568 | tf_op jit(solution)/shard_map/ppermute | solution.py:46
  104.7 0.6 constant_dynamic-update-slice_fusion.8
  105.3 5.8 %collective-permute-done.8 = bf16[256,128]{0,1:T(8,128)(2,1)S(1)} collective-permute-done((bf16[256,128]{0,1:T(8,128)(2,1)S(1)}, bf16[256,128]{0,1:T(8,128)(2,1)S(1)}, u32[]{:S(2)}, u32[]{:S(2)}) %collective-permute-start.8) | collective-permute-done | bytes 65568 | tf_op jit(solution)/shard_map/ppermute | solution.py:46
  111.7 6.9 %collective-permute-done.9 = bf16[256,128]{0,1:T(8,128)(2,1)S(1)} collective-permute-done((bf16[256,128]{0,1:T(8,128)(2,1)S(1)}, bf16[256,128]{0,1:T(8,128)(2,1)S(1)}, u32[]{:S(2)}, u32[]{:S(2)}) %collective-permute-start.9) | collective-permute-done | bytes 65568 | tf_op jit(solution)/shard_map/ppermute | solution.py:46
  119.2 6.1 %collective-permute-done.10 = bf16[256,128]{0,1:T(8,128)(2,1)S(1)} collective-permute-done((bf16[256,128]{0,1:T(8,128)(2,1)S(1)}, bf16[256,128]{0,1:T(8,128)(2,1)S(1)}, u32[]{:S(2)}, u32[]{:S(2)}) %collective-permute-start.10) | collective-permute-done | bytes 65568 | tf_op jit(solution)/shard_map/ppermute | solution.py:46
  126.0 5.8 %collective-permute-done.11 = bf16[256,128]{0,1:T(8,128)(2,1)S(1)} collective-permute-done((bf16[256,128]{0,1:T(8,128)(2,1)S(1)}, bf16[256,128]{0,1:T(8,128)(2,1)S(1)}, u32[]{:S(2)}, u32[]{:S(2)}) %collective-permute-start.11) | collective-permute-done | bytes 65568 | tf_op jit(solution)/shard_map/ppermute | solution.py:46
  132.4 5.8 %collective-permute-done.12 = bf16[256,128]{0,1:T(8,128)(2,1)S(1)} collective-permute-done((bf16[256,128]{0,1:T(8,128)(2,1)S(1)}, bf16[256,128]{0,1:T(8,128)(2,1)S(1)}, u32[]{:S(2)}, u32[]{:S(2)}) %collective-permute-start.12) | collective-permute-done | bytes 65568 | tf_op jit(solution)/shard_map/ppermute | solution.py:46
  138.8 5.8 %collective-permute-done.13 = bf16[256,128]{0,1:T(8,128)(2,1)S(1)} collective-permute-done((bf16[256,128]{0,1:T(8,128)(2,1)S(1)}, bf16[256,128]{0,1:T(8,128)(2,1)S(1)}, u32[]{:S(2)}, u32[]{:S(2)}) %collective-permute-start.13) | collective-permute-done | bytes 65568 | tf_op jit(solution)/shard_map/ppermute | solution.py:46
  145.2 5.8 %collective-permute-done.14 = bf16[256,128]{0,1:T(8,128)(2,1)S(1)} collective-permute-done((bf16[256,128]{0,1:T(8,128)(2,1)S(1)}, bf16[256,128]{0,1:T(8,128)(2,1)S(1)}, u32[]{:S(2)}, u32[]{:S(2)}) %collective-permute-start.14) | collective-permute-done | bytes 65568 | tf_op jit(solution)/shard_map/ppermute | solution.py:46
  151.5 5.8 %collective-permute-done.15 = bf16[256,128]{0,1:T(8,128)(2,1)S(1)} collective-permute-done((bf16[256,128]{0,1:T(8,128)(2,1)S(1)}, bf16[256,128]{0,1:T(8,128)(2,1)S(1)}, u32[]{:S(2)}, u32[]{:S(2)}) %collective-permute-start.15) | collective-permute-done | bytes 65568 | tf_op jit(solution)/shard_map/ppermute | solution.py:46
  158.0 29.1 %convolution_convert_fusion = bf16[1,128,4096]{2,0,1:T(2,128)(2,1)S(1)} fusion(bf16[1,255,4096]{2,1,0:T(8,128)(2,1)S(1)} %pad_maximum_fusion, bf16[128,1,4096]{2,0,1:T(8,128)(2,1)} %bitcast.2), kind=kOutput, calls=%fused_computation | convolution fusion | flops 134742016 | bytes 4186112 | tf_op jit(solution)/shard_map/conv_general_dilated | solution.py:15
  187.1 2.1 %copy.52 = bf16[1,128,4096]{2,1,0:T(8,128)(2,1)} copy(bf16[1,128,4096]{2,0,1:T(2,128)(2,1)S(1)} %convolution_convert_fusion) | data formatting | bytes 2097152
  189.2 1.7 copy.53
  (36 shorter events, 7.2 us)
Async XLA Ops:
  7.2 7.6 %copy-start = (bf16[1,128,4096]{2,1,0:T(8,128)(2,1)S(1)}, bf16[1,128,4096]{2,1,0:T(8,128)(2,1)}, u32[]{:S(2)}) copy-start(bf16[1,128,4096]{2,1,0:T(8,128)(2,1)} %param.7) | copy-start | bytes 3145732
  7.2 150.8 %reduce-scatter.2.cloned.1.call-start = ((), (), s32[]{:S(2)}) async-start(), calls=%async_computation.1 | async-start | bytes 2228224 | tf_op jit(solution)/shard_map/reduce_scatter | solution.py:49
  10.0 4.6 %collective-permute-start = (bf16[1,127,4096]{2,1,0:T(8,128)(2,1)S(1)}, bf16[1,127,4096]{2,1,0:T(8,128)(2,1)S(1)}, u32[]{:S(2)}, u32[]{:S(2)}) collective-permute-start(bf16[1,127,4096]{2,1,0:T(8,128)(2,1)S(1)} %bitcast.14), channel_id=1, source_target_pairs={{1,0},{2,1},{3,2},{4,3},{5,4},{6,5},{7,6},{8,7},{9,8},{10,9},{11,1... | collective-permute-start | bytes 3121160 | tf_op jit(solution)/shard_map/ppermute | solution.py:10
  48.3 0.8 copy-start.1
  48.3 140.9 %all-reduce.2.cloned.1.call-start = ((), (), s32[]{:S(2)}) async-start(), calls=%async_computation.2 | async-start | bytes 262144 | tf_op jit(solution)/shard_map/psum | solution.py:52
  49.2 14.7 %collective-permute-start.1 = (bf16[256,128]{0,1:T(8,128)(2,1)S(1)}, bf16[256,128]{0,1:T(8,128)(2,1)S(1)}, u32[]{:S(2)}, u32[]{:S(2)}) collective-permute-start(bf16[256,128]{0,1:T(8,128)(2,1)S(1)} %copy.46), channel_id=1, source_target_pairs={{0,1},{1,2},{2,3},{3,4},{4,5},{5,6},{6,7},{7,8},{8,9},{9,10},{10,1... | collective-permute-start | bytes 196616 | tf_op jit(solution)/shard_map/ppermute | solution.py:46
  63.9 6.4 %collective-permute-start.2 = (bf16[256,128]{0,1:T(8,128)(2,1)S(1)}, bf16[256,128]{0,1:T(8,128)(2,1)S(1)}, u32[]{:S(2)}, u32[]{:S(2)}) collective-permute-start(bf16[256,128]{0,1:T(8,128)(2,1)S(1)} %collective-permute-done.1), channel_id=1, source_target_pairs={{0,1},{1,2},{2,3},{3,4},{4,5},{5,6},{6,7},{7,8},{8,9},{9,10},{10,1... | collective-permute-start | bytes 196616 | tf_op jit(solution)/shard_map/ppermute | solution.py:46
  70.3 6.4 %collective-permute-start.3 = (bf16[256,128]{0,1:T(8,128)(2,1)S(1)}, bf16[256,128]{0,1:T(8,128)(2,1)S(1)}, u32[]{:S(2)}, u32[]{:S(2)}) collective-permute-start(bf16[256,128]{0,1:T(8,128)(2,1)S(1)} %collective-permute-done.2), channel_id=1, source_target_pairs={{0,1},{1,2},{2,3},{3,4},{4,5},{5,6},{6,7},{7,8},{8,9},{9,10},{10,1... | collective-permute-start | bytes 196616 | tf_op jit(solution)/shard_map/ppermute | solution.py:46
  76.7 6.4 %collective-permute-start.4 = (bf16[256,128]{0,1:T(8,128)(2,1)S(1)}, bf16[256,128]{0,1:T(8,128)(2,1)S(1)}, u32[]{:S(2)}, u32[]{:S(2)}) collective-permute-start(bf16[256,128]{0,1:T(8,128)(2,1)S(1)} %collective-permute-done.3), channel_id=1, source_target_pairs={{0,1},{1,2},{2,3},{3,4},{4,5},{5,6},{6,7},{7,8},{8,9},{9,10},{10,1... | collective-permute-start | bytes 196616 | tf_op jit(solution)/shard_map/ppermute | solution.py:46
  83.1 6.4 %collective-permute-start.5 = (bf16[256,128]{0,1:T(8,128)(2,1)S(1)}, bf16[256,128]{0,1:T(8,128)(2,1)S(1)}, u32[]{:S(2)}, u32[]{:S(2)}) collective-permute-start(bf16[256,128]{0,1:T(8,128)(2,1)S(1)} %collective-permute-done.4), channel_id=1, source_target_pairs={{0,1},{1,2},{2,3},{3,4},{4,5},{5,6},{6,7},{7,8},{8,9},{9,10},{10,1... | collective-permute-start | bytes 196616 | tf_op jit(solution)/shard_map/ppermute | solution.py:46
  89.5 7.6 %collective-permute-start.6 = (bf16[256,128]{0,1:T(8,128)(2,1)S(1)}, bf16[256,128]{0,1:T(8,128)(2,1)S(1)}, u32[]{:S(2)}, u32[]{:S(2)}) collective-permute-start(bf16[256,128]{0,1:T(8,128)(2,1)S(1)} %collective-permute-done.5), channel_id=1, source_target_pairs={{0,1},{1,2},{2,3},{3,4},{4,5},{5,6},{6,7},{7,8},{8,9},{9,10},{10,1... | collective-permute-start | bytes 196616 | tf_op jit(solution)/shard_map/ppermute | solution.py:46
  97.1 7.6 %collective-permute-start.7 = (bf16[256,128]{0,1:T(8,128)(2,1)S(1)}, bf16[256,128]{0,1:T(8,128)(2,1)S(1)}, u32[]{:S(2)}, u32[]{:S(2)}) collective-permute-start(bf16[256,128]{0,1:T(8,128)(2,1)S(1)} %collective-permute-done.6), channel_id=1, source_target_pairs={{0,1},{1,2},{2,3},{3,4},{4,5},{5,6},{6,7},{7,8},{8,9},{9,10},{10,1... | collective-permute-start | bytes 196616 | tf_op jit(solution)/shard_map/ppermute | solution.py:46
  104.7 6.4 %collective-permute-start.8 = (bf16[256,128]{0,1:T(8,128)(2,1)S(1)}, bf16[256,128]{0,1:T(8,128)(2,1)S(1)}, u32[]{:S(2)}, u32[]{:S(2)}) collective-permute-start(bf16[256,128]{0,1:T(8,128)(2,1)S(1)} %collective-permute-done.7), channel_id=1, source_target_pairs={{0,1},{1,2},{2,3},{3,4},{4,5},{5,6},{6,7},{7,8},{8,9},{9,10},{10,1... | collective-permute-start | bytes 196616 | tf_op jit(solution)/shard_map/ppermute | solution.py:46
  111.1 7.5 %collective-permute-start.9 = (bf16[256,128]{0,1:T(8,128)(2,1)S(1)}, bf16[256,128]{0,1:T(8,128)(2,1)S(1)}, u32[]{:S(2)}, u32[]{:S(2)}) collective-permute-start(bf16[256,128]{0,1:T(8,128)(2,1)S(1)} %collective-permute-done.8), channel_id=1, source_target_pairs={{0,1},{1,2},{2,3},{3,4},{4,5},{5,6},{6,7},{7,8},{8,9},{9,10},{10,1... | collective-permute-start | bytes 196616 | tf_op jit(solution)/shard_map/ppermute | solution.py:46
  118.6 6.8 %collective-permute-start.10 = (bf16[256,128]{0,1:T(8,128)(2,1)S(1)}, bf16[256,128]{0,1:T(8,128)(2,1)S(1)}, u32[]{:S(2)}, u32[]{:S(2)}) collective-permute-start(bf16[256,128]{0,1:T(8,128)(2,1)S(1)} %collective-permute-done.9), channel_id=1, source_target_pairs={{0,1},{1,2},{2,3},{3,4},{4,5},{5,6},{6,7},{7,8},{8,9},{9,10},{10,1... | collective-permute-start | bytes 196616 | tf_op jit(solution)/shard_map/ppermute | solution.py:46
  125.4 6.4 %collective-permute-start.11 = (bf16[256,128]{0,1:T(8,128)(2,1)S(1)}, bf16[256,128]{0,1:T(8,128)(2,1)S(1)}, u32[]{:S(2)}, u32[]{:S(2)}) collective-permute-start(bf16[256,128]{0,1:T(8,128)(2,1)S(1)} %collective-permute-done.10), channel_id=1, source_target_pairs={{0,1},{1,2},{2,3},{3,4},{4,5},{5,6},{6,7},{7,8},{8,9},{9,10},{10,1... | collective-permute-start | bytes 196616 | tf_op jit(solution)/shard_map/ppermute | solution.py:46
  131.7 6.4 %collective-permute-start.12 = (bf16[256,128]{0,1:T(8,128)(2,1)S(1)}, bf16[256,128]{0,1:T(8,128)(2,1)S(1)}, u32[]{:S(2)}, u32[]{:S(2)}) collective-permute-start(bf16[256,128]{0,1:T(8,128)(2,1)S(1)} %collective-permute-done.11), channel_id=1, source_target_pairs={{0,1},{1,2},{2,3},{3,4},{4,5},{5,6},{6,7},{7,8},{8,9},{9,10},{10,1... | collective-permute-start | bytes 196616 | tf_op jit(solution)/shard_map/ppermute | solution.py:46
  138.1 6.4 %collective-permute-start.13 = (bf16[256,128]{0,1:T(8,128)(2,1)S(1)}, bf16[256,128]{0,1:T(8,128)(2,1)S(1)}, u32[]{:S(2)}, u32[]{:S(2)}) collective-permute-start(bf16[256,128]{0,1:T(8,128)(2,1)S(1)} %collective-permute-done.12), channel_id=1, source_target_pairs={{0,1},{1,2},{2,3},{3,4},{4,5},{5,6},{6,7},{7,8},{8,9},{9,10},{10,1... | collective-permute-start | bytes 196616 | tf_op jit(solution)/shard_map/ppermute | solution.py:46
  144.5 6.4 %collective-permute-start.14 = (bf16[256,128]{0,1:T(8,128)(2,1)S(1)}, bf16[256,128]{0,1:T(8,128)(2,1)S(1)}, u32[]{:S(2)}, u32[]{:S(2)}) collective-permute-start(bf16[256,128]{0,1:T(8,128)(2,1)S(1)} %collective-permute-done.13), channel_id=1, source_target_pairs={{0,1},{1,2},{2,3},{3,4},{4,5},{5,6},{6,7},{7,8},{8,9},{9,10},{10,1... | collective-permute-start | bytes 196616 | tf_op jit(solution)/shard_map/ppermute | solution.py:46
  150.9 6.4 %collective-permute-start.15 = (bf16[256,128]{0,1:T(8,128)(2,1)S(1)}, bf16[256,128]{0,1:T(8,128)(2,1)S(1)}, u32[]{:S(2)}, u32[]{:S(2)}) collective-permute-start(bf16[256,128]{0,1:T(8,128)(2,1)S(1)} %collective-permute-done.14), channel_id=1, source_target_pairs={{0,1},{1,2},{2,3},{3,4},{4,5},{5,6},{6,7},{7,8},{8,9},{9,10},{10,1... | collective-permute-start | bytes 196616 | tf_op jit(solution)/shard_map/ppermute | solution.py:46
Sparse Core Ops, SparseCore 0:
  48.4 76.1 reduce-scatter.1
  158.1 18.6 all-reduce.1
